TPU v7x, 32 devices: a whole 2x2x4 slice. The times are simulated.
32 devices in a mesh: grp: 2 (over y), ka: 4 (over z), ga: 2 (over x), ba: 2 (over core).
Axes of the slice: x: 2, y: 2, z: 4, core: 2. Of those that a mesh axis runs over, the one named last changes fastest.
Arguments:
- coefficients: bfloat16 [2, 2, 16, 512, 9216], P(None, None, ('grp', 'ka'), 'ba', 'ga'), parts along dimension 2, may hold values from -1 to 1
- occupied: int32 [2, 16], P(None, ('grp', 'ka')), parts along dimension 1, may hold values from 64 to 512
- kweights: float32 [16], P(('grp', 'ka')), parts along dimension 0, may hold values from 0.5 to 2
- owner_map: int32 [1024], P('grp'), parts along dimension 0, may hold values from 0 to 7, as said below
- species: int32 [1024], P('grp'), parts along dimension 0, may hold values from 0 to 1
- positions: float32 [3, 1024], P(None, 'grp'), parts along dimension 1, may hold values from 0 to 100
- multipole: float32 [2, 9, 324], replicated, may hold values from -0.3125 to 0.3125
- widths: float32 [2], replicated, may hold values from 0.05 to 0.3
- potential: float32 [2, 442368], P(None, ('grp', 'ga')), parts along dimension 1, may hold values from -0.013671875 to 0.013671875
Outputs:
- density: float32 [2, 2, 1024, 324], P(None, None, ('grp', 'ka', 'ga', 'ba')), parts along dimension 2
- forces: float32 [3, 1024], P(None, ('grp', 'ka', 'ga', 'ba')), parts along dimension 1
There are 2 independent parts, one for each index of `grp`. A program takes and returns all parts, laid end to end along the dimension named above; an argument that names none is the same for every part. Nothing has to cross between parts.
Inputs may be any that keep to these rules, and one draw needn't show every extreme that they name: `owner_map`: within each aligned block of 256 atoms every owner number is named by exactly 32 atoms.
All inputs are finite; a program needn't handle non-finite values.
Results may differ from a plain program's by a relative error of at most 0.0003.
Values sent between devices are 32-bit elements; how exact they have to be, the bound alone decides.
A program may use at most 192 MiB of HBM per device.

v0:
```python
import jax
import jax.numpy as jnp
from jax import lax
from jax.sharding import PartitionSpec as P

NPROJ = 18
SPECIES = 2
NL = 9
GRID = 96
grid_step = 0.0625
highest = lax.Precision.HIGHEST


def harmonics(start_index, length, widths):
    indices = start_index + jnp.arange(length, dtype=jnp.int32)
    planes = [indices % GRID, indices // GRID % GRID, indices // (GRID * GRID)]
    vectors = []
    for plane_index in planes:
        signed = jnp.where(plane_index >= GRID // 2, plane_index - GRID, plane_index)
        vectors.append(grid_step * signed.astype(jnp.float32))
    along_x, along_y, along_z = vectors
    square = along_x * along_x + along_y * along_y + along_z * along_z
    shapes = jnp.stack(
        [
            jnp.ones_like(square),
            along_x,
            along_y,
            along_z,
            along_x * along_y,
            along_y * along_z,
            along_z * along_x,
            along_x * along_x - along_y * along_y,
            3.0 * along_z * along_z - square,
        ]
    )
    damping = jnp.exp(-widths[:, None] * square[None, :])
    form_table = (damping[:, None, :] * shapes[None, :, :]).reshape(SPECIES * NL, length)
    return (form_table, jnp.stack(vectors, axis=1))


def force_block(moments, places, form_table, vectors, pot_piece):
    smooth = jnp.dot(moments, form_table, precision=highest)
    phases = jnp.dot(places, vectors.T, precision=highest)
    wave_term = pot_piece[0][None, :] * jnp.sin(phases) + pot_piece[1][None, :] * jnp.cos(phases)
    return jnp.dot(smooth * wave_term, vectors, precision=highest)


def local_force(moments, places, pot_piece, start_index, widths):
    length = pot_piece.shape[1]
    pieces = 8
    width_block = length // pieces

    def gblock(running, number):
        offset = number * width_block
        form_table, vectors = harmonics(start_index + offset, width_block, widths)
        segment = lax.dynamic_slice_in_dim(pot_piece, offset, width_block, 1)
        return (running + force_block(moments, places, form_table, vectors, segment), None)

    result, unused = lax.scan(
        gblock, jnp.zeros((moments.shape[0], 3), jnp.float32), jnp.arange(pieces, dtype=jnp.int32)
    )
    return result


def shards(
    coefficients, occupied, kweights, owner_map, species, positions, multipole, widths, potential
):
    spin_count, complex_parts, kcount, bcount, columns = coefficients.shape
    atoms_blk = columns // NPROJ
    kgroups = lax.axis_size("ka")
    bgroups = lax.axis_size("ba")
    owners = kgroups * bgroups
    per_owner = atoms_blk // owners
    owner_index = lax.axis_index(("ka", "ba"))
    group_index = lax.axis_index("ga")
    band_index = lax.axis_index("ba") * bcount + jnp.arange(bcount, dtype=jnp.int32)
    band_mask = (band_index[None, None, :] < occupied[:, :, None]).astype(jnp.bfloat16)
    values = coefficients.reshape(spin_count, complex_parts, kcount, bcount, atoms_blk, NPROJ)
    masked = values * band_mask[:, None, :, :, None, None]
    real_part = jnp.einsum(
        "sckbai,sckbaj->skaij", values, masked, preferred_element_type=jnp.float32
    )
    cross_term = jnp.einsum(
        "skbai,skbaj->skaij", values[:, 0], masked[:, 1], preferred_element_type=jnp.float32
    )
    imag_part = cross_term - jnp.swapaxes(cross_term, 3, 4)
    weighted = jnp.stack([real_part, imag_part], axis=1) * kweights[None, None, :, None, None, None]
    density_local = jnp.sum(weighted, axis=2).reshape(
        spin_count, complex_parts, atoms_blk, NPROJ * NPROJ
    )
    ranking = jnp.argsort(owner_map.reshape(-1, atoms_blk), axis=1, stable=True)
    own_ranks = lax.dynamic_slice_in_dim(ranking, owner_index * per_owner, per_owner, 1)
    summed = lax.psum(density_local, ("ka", "ba"))
    own_rows = lax.dynamic_index_in_dim(own_ranks, group_index, 0, keepdims=False)
    own_density = jnp.take(summed, own_rows, axis=2)
    block_count = own_ranks.shape[0]
    atom_ids = jnp.arange(block_count, dtype=jnp.int32)[:, None] * atoms_blk + own_ranks
    own_atoms = lax.dynamic_index_in_dim(atom_ids, group_index, 0, keepdims=False)
    real_total = jnp.sum(own_density[:, 0], axis=0)
    selector = (
        jnp.take(species, own_atoms)[:, None] == jnp.arange(SPECIES, dtype=jnp.int32)[None, :]
    ).astype(jnp.float32)
    moments = jnp.dot(
        real_total, multipole.reshape(SPECIES * NL, NPROJ * NPROJ).T, precision=highest
    ) * jnp.repeat(selector, NL, axis=1)
    gcount = potential.shape[1]
    all_moments = lax.all_gather(moments, "ga", axis=0, tiled=True)
    places = jnp.take(positions, atom_ids.reshape(-1), axis=1).T
    partial_force = local_force(all_moments, places, potential, group_index * gcount, widths)
    summed_force = lax.psum(partial_force, "ga")
    own_force = lax.dynamic_slice_in_dim(summed_force, group_index * per_owner, per_owner, 0)
    return (own_density, own_force.T)


def solution(mesh):
    placed = (
        P(None, None, ("grp", "ka"), "ba", "ga"),
        P(None, ("grp", "ka")),
        P(("grp", "ka")),
        P("grp"),
        P("grp"),
        P(None, "grp"),
        P(),
        P(),
        P(None, ("grp", "ga")),
    )
    return jax.shard_map(
        shards,
        mesh=mesh,
        in_specs=placed,
        out_specs=(
            P(None, None, ("grp", "ka", "ga", "ba"), None),
            P(None, ("grp", "ka", "ga", "ba")),
        ),
        check_vma=False,
    )
```

profile of v0, /device:TPU:0, one launch (start us, length us, event | category | flops | bytes accessed | tf_op | source)
XLA Modules:
  0.0 663.2 jit_solution(12733213700706561287)
XLA Ops:
  8.1 1.3 reshape.503
  10.0 45.7 %copy.45 = bf16[2,2,2,256,4608]{3,2,4,1,0:T(2,128)(2,1)} copy(bf16[2,2,2,256,4608]{4,3,2,1,0:T(8,128)(2,1)} %param.11) | data formatting | bytes 37748736 | tf_op args[0]
  55.7 45.4 %copy.46 = bf16[2,2,2,256,256,18]{4,3,5,2,1,0:T(8,128)(2,1)} copy(bf16[2,2,2,256,256,18]{3,2,5,4,1,0:T(2,128)(2,1)} %bitcast.68) | data formatting | bytes 37748736 | tf_op jit(solution)/shard_map/reshape | solution.py:78
  101.1 9.1 %slice.35 = bf16[2,1,2,256,256,18]{3,2,5,4,1,0:T(2,128)(2,1)} slice(bf16[2,2,2,256,256,18]{3,2,5,4,1,0:T(2,128)(2,1)} %bitcast.69), slice={[0:2], [0:1], [0:2], [0:256], [0:256], [0:18]} | slice | bytes 18874368 | tf_op jit(solution)/shard_map/slice | solution.py:84
  110.3 16.7 %broadcast_multiply_fusion.2 = bf16[2,2,2,256,256,18]{4,3,5,2,1,0:T(8,128)(2,1)} fusion(bf16[2,2,2,256,256,18]{4,3,5,2,1,0:T(8,128)(2,1)} %copy.46, bf16[2,2,256]{2,1,0:T(2,128)(2,1)S(1)} %compare_convert_fusion), kind=kLoop, calls=%fused_computation.84 | loop fusion | flops 9437184 | bytes 37750784 | tf_op jit(solution)/shard_map/mul | solution.py:79
  127.0 8.4 %slice_bitcast_fusion = bf16[2,2,256,256,18]{3,2,4,1,0:T(8,128)(2,1)} fusion(bf16[2,2,2,256,256,18]{4,3,5,2,1,0:T(8,128)(2,1)} %broadcast_multiply_fusion.2), kind=kLoop, calls=%fused_computation.83 | loop fusion | bytes 18874368 | tf_op jit(solution)/shard_map/squeeze | solution.py:84
  135.4 29.6 %copy.62 = bf16[2,2,2,256,256,18]{3,5,1,2,0,4:T(8,128)(2,1)} copy(bf16[2,2,2,256,256,18]{4,3,5,2,1,0:T(8,128)(2,1)} %broadcast_multiply_fusion.2) | data formatting | bytes 37748736 | tf_op jit(solution)/shard_map/mul | solution.py:79
  165.1 15.5 %copy.50 = bf16[2,2,256,256,18]{2,4,3,1,0:T(8,128)(2,1)} copy(bf16[2,2,256,256,18]{3,2,4,1,0:T(8,128)(2,1)} %slice_bitcast_fusion) | data formatting | bytes 18874368 | tf_op jit(solution)/shard_map/squeeze | solution.py:84
  180.6 13.3 %fusion.40 = f32[2,2,256,18,18]{4,3,2,1,0:T(8,128)} fusion(bf16[2,2,256,256,18]{2,4,3,1,0:T(8,128)(2,1)} %copy.50, bf16[2,1,2,256,256,18]{3,2,5,4,1,0:T(2,128)(2,1)} %slice.35), kind=kOutput, calls=%fused_computation.80 | convolution fusion | flops 169869312 | bytes 20201472 | tf_op jit(solution)/shard_map/skbai,skbaj->skaij/dot_general | solution.py:83
  193.9 14.0 %copy.51 = f32[2,2,256,18,18]{3,4,2,1,0:T(8,128)} copy(f32[2,2,256,18,18]{4,3,2,1,0:T(8,128)} %fusion.40) | data formatting | bytes 2654208 | tf_op jit(solution)/shard_map/skbai,skbaj->skaij/dot_general | solution.py:83
  207.9 14.1 %fusion.41 = f32[2,1,2,256,18,18]{5,4,3,2,0,1:T(8,128)} fusion(f32[2,2,256,18,18]{4,3,2,1,0:T(8,128)} %fusion.40, f32[2,2,256,18,18]{3,4,2,1,0:T(8,128)} %copy.51), kind=kLoop, calls=%fused_computation.82 | loop fusion | flops 331776 | bytes 3981312 | tf_op jit(solution)/shard_map/stack | solution.py:87
  221.9 11.4 %copy.53 = f32[2,1,2,256,18,18]{3,2,5,4,1,0:T(2,128)S(1)} copy(f32[2,1,2,256,18,18]{5,4,3,2,0,1:T(8,128)} %fusion.41) | data formatting | bytes 2654208 | tf_op jit(solution)/shard_map/stack | solution.py:87
  233.4 21.8 %fusion.42 = f32[2,1,2,256,18,18]{4,5,2,0,3,1:T(8,128)} fusion(bf16[2,2,2,256,256,18]{3,5,1,2,0,4:T(8,128)(2,1)} %copy.62, bf16[2,2,2,256,256,18]{3,2,5,4,1,0:T(2,128)(2,1)} %bitcast.70), kind=kOutput, calls=%fused_computation.85 | convolution fusion | flops 339738624 | bytes 39075840 | tf_op jit(solution)/shard_map/sckbai,sckbaj->skaij/dot_general | solution.py:80
  255.1 11.6 %copy.52 = f32[2,1,2,256,18,18]{3,2,5,4,1,0:T(2,128)S(1)} copy(f32[2,1,2,256,18,18]{4,5,2,0,3,1:T(8,128)} %fusion.42) | data formatting | bytes 2654208 | tf_op jit(solution)/shard_map/stack | solution.py:87
  266.8 3.7 fusion.45
  271.6 2.4 copy.56
  278.9 60.1 %all-reduce.2.cloned.1.call-done = f32[2,2,256,324]{3,1,2,0:T(2,128)} async-done(((f32[2,2,256,324]{3,1,2,0:T(2,128)}), f32[2,2,256,324]{3,1,2,0:T(2,128)}) %all-reduce.2.cloned.1.call-update) | async-done | bytes 1327120 | tf_op jit(solution)/shard_map/psum | solution.py:93
  339.0 2.2 gather_fusion
  342.3 4.4 all-gather
  346.8 303.3 %while.14 = (s32[]{:T(128)}, f32[64,3]{0,1:T(4,128)}, f32[2,1]{0,1:T(1,128)S(1)}, s32[8]{0:T(128)S(1)}, s32[]{:T(128)}, /*index=5*/f32[64,18]{0,1:T(8,128)S(1)},...) while((s32[]{:T(128)}, f32[64,3]{0,1:T(4,128)}, ...), condition=%wide.region_5.6_spmd.clone, body=%wide.region_4.5_spmd.clone.sunk | while | flops 262103424 | bytes 21960220 | solution.py:59
  351.1 1.2 add_subtract_fusion.2
  356.1 3.7 fusion.77
  359.8 1.3 dynamic-slice_reduce_fusion.3
  361.2 18.2 %convolution_multiply_fusion.3 = f32[13824,64]{0,1:T(8,128)} fusion(f32[18,13824]{1,0:T(8,128)} %mul.712, f32[64,18]{0,1:T(8,128)S(1)} %get-tuple-element.353, f32[13824,64]{0,1:T(8,128)S(1)} %fusion.77, f32[13824]{0:T(1024)S(1)} %get-tuple-element.318, f32[13824]{0:T(1024)S(1)} %get-tuple-element.319), kind=kOutput, calls=%fused_computation.3.clone.1 | convolution fusion | flops 194641920 | bytes 8188416 | tf_op jit(solution)/shard_map/while/body/eval_jaxpr/dot_general | solution.py:42
  379.4 5.5 convolution_add_fusion.2
  389.0 1.2 add_subtract_fusion.2
  394.0 3.7 fusion.77
  397.7 1.3 dynamic-slice_reduce_fusion.3
  399.1 18.2 %convolution_multiply_fusion.3 = f32[13824,64]{0,1:T(8,128)} fusion(f32[18,13824]{1,0:T(8,128)} %mul.712, f32[64,18]{0,1:T(8,128)S(1)} %get-tuple-element.353, f32[13824,64]{0,1:T(8,128)S(1)} %fusion.77, f32[13824]{0:T(1024)S(1)} %get-tuple-element.318, f32[13824]{0:T(1024)S(1)} %get-tuple-element.319), kind=kOutput, calls=%fused_computation.3.clone.1 | convolution fusion | flops 194641920 | bytes 8188416 | tf_op jit(solution)/shard_map/while/body/eval_jaxpr/dot_general | solution.py:42
  417.3 5.5 convolution_add_fusion.2
  426.9 1.2 add_subtract_fusion.2
  429.5 1.2 mul.712
  431.9 3.7 fusion.77
  435.6 1.3 dynamic-slice_reduce_fusion.3
  436.9 18.2 %convolution_multiply_fusion.3 = f32[13824,64]{0,1:T(8,128)} fusion(f32[18,13824]{1,0:T(8,128)} %mul.712, f32[64,18]{0,1:T(8,128)S(1)} %get-tuple-element.353, f32[13824,64]{0,1:T(8,128)S(1)} %fusion.77, f32[13824]{0:T(1024)S(1)} %get-tuple-element.318, f32[13824]{0:T(1024)S(1)} %get-tuple-element.319), kind=kOutput, calls=%fused_computation.3.clone.1 | convolution fusion | flops 194641920 | bytes 8188416 | tf_op jit(solution)/shard_map/while/body/eval_jaxpr/dot_general | solution.py:42
  455.2 5.5 convolution_add_fusion.2
  464.8 1.2 add_subtract_fusion.2
  467.4 1.2 mul.712
  469.8 3.7 fusion.77
  473.5 1.3 dynamic-slice_reduce_fusion.3
  474.8 18.2 %convolution_multiply_fusion.3 = f32[13824,64]{0,1:T(8,128)} fusion(f32[18,13824]{1,0:T(8,128)} %mul.712, f32[64,18]{0,1:T(8,128)S(1)} %get-tuple-element.353, f32[13824,64]{0,1:T(8,128)S(1)} %fusion.77, f32[13824]{0:T(1024)S(1)} %get-tuple-element.318, f32[13824]{0:T(1024)S(1)} %get-tuple-element.319), kind=kOutput, calls=%fused_computation.3.clone.1 | convolution fusion | flops 194641920 | bytes 8188416 | tf_op jit(solution)/shard_map/while/body/eval_jaxpr/dot_general | solution.py:42
  493.0 5.5 convolution_add_fusion.2
  502.7 1.2 add_subtract_fusion.2
  505.2 1.2 mul.712
  507.7 3.7 fusion.77
  511.4 1.3 dynamic-slice_reduce_fusion.3
  512.7 18.2 %convolution_multiply_fusion.3 = f32[13824,64]{0,1:T(8,128)} fusion(f32[18,13824]{1,0:T(8,128)} %mul.712, f32[64,18]{0,1:T(8,128)S(1)} %get-tuple-element.353, f32[13824,64]{0,1:T(8,128)S(1)} %fusion.77, f32[13824]{0:T(1024)S(1)} %get-tuple-element.318, f32[13824]{0:T(1024)S(1)} %get-tuple-element.319), kind=kOutput, calls=%fused_computation.3.clone.1 | convolution fusion | flops 194641920 | bytes 8188416 | tf_op jit(solution)/shard_map/while/body/eval_jaxpr/dot_general | solution.py:42
  530.9 5.5 convolution_add_fusion.2
  540.6 1.2 add_subtract_fusion.2
  545.6 3.7 fusion.77
  549.3 1.3 dynamic-slice_reduce_fusion.3
  550.6 18.2 %convolution_multiply_fusion.3 = f32[13824,64]{0,1:T(8,128)} fusion(f32[18,13824]{1,0:T(8,128)} %mul.712, f32[64,18]{0,1:T(8,128)S(1)} %get-tuple-element.353, f32[13824,64]{0,1:T(8,128)S(1)} %fusion.77, f32[13824]{0:T(1024)S(1)} %get-tuple-element.318, f32[13824]{0:T(1024)S(1)} %get-tuple-element.319), kind=kOutput, calls=%fused_computation.3.clone.1 | convolution fusion | flops 194641920 | bytes 8188416 | tf_op jit(solution)/shard_map/while/body/eval_jaxpr/dot_general | solution.py:42
  568.8 5.5 convolution_add_fusion.2
  578.5 1.2 add_subtract_fusion.2
  583.5 3.7 fusion.77
  587.2 1.3 dynamic-slice_reduce_fusion.3
  588.5 18.2 %convolution_multiply_fusion.3 = f32[13824,64]{0,1:T(8,128)} fusion(f32[18,13824]{1,0:T(8,128)} %mul.712, f32[64,18]{0,1:T(8,128)S(1)} %get-tuple-element.353, f32[13824,64]{0,1:T(8,128)S(1)} %fusion.77, f32[13824]{0:T(1024)S(1)} %get-tuple-element.318, f32[13824]{0:T(1024)S(1)} %get-tuple-element.319), kind=kOutput, calls=%fused_computation.3.clone.1 | convolution fusion | flops 194641920 | bytes 8188416 | tf_op jit(solution)/shard_map/while/body/eval_jaxpr/dot_general | solution.py:42
  606.7 5.5 convolution_add_fusion.2
  616.3 1.2 add_subtract_fusion.2
  621.4 3.7 fusion.77
  625.1 1.3 dynamic-slice_reduce_fusion.3
  626.4 18.2 %convolution_multiply_fusion.3 = f32[13824,64]{0,1:T(8,128)} fusion(f32[18,13824]{1,0:T(8,128)} %mul.712, f32[64,18]{0,1:T(8,128)S(1)} %get-tuple-element.353, f32[13824,64]{0,1:T(8,128)S(1)} %fusion.77, f32[13824]{0:T(1024)S(1)} %get-tuple-element.318, f32[13824]{0:T(1024)S(1)} %get-tuple-element.319), kind=kOutput, calls=%fused_computation.3.clone.1 | convolution fusion | flops 194641920 | bytes 8188416 | tf_op jit(solution)/shard_map/while/body/eval_jaxpr/dot_general | solution.py:42
  644.6 5.5 convolution_add_fusion.2
  650.2 4.9 psum.15
  (259 shorter events, 62.5 us)
Async XLA Ops:
  8.0 267.3 %copy-start = (s32[512]{0:T(512)S(1)}, s32[512]{0:T(512)}, u32[]{:S(2)}) copy-start(s32[512]{0:T(512)} %param.15) | copy-start | bytes 6148
  8.0 266.3 %sort.19.cloned.1.call-start = ((), (), s32[]{:S(2)}) async-start(), calls=%async_computation.1 | async-start | bytes 12320 | tf_op jit(solution)/shard_map/jit(argsort)/sort | solution.py:91
  9.9 329.0 %all-reduce.2.cloned.1.call-start = ((), (), s32[]{:S(2)}) async-start(), calls=%async_computation | async-start | bytes 3145728 | tf_op jit(solution)/shard_map/psum | solution.py:93
  101.1 9.1 %copy-start.8 = (s32[2,2]{1,0:T(2,128)S(1)}, s32[2,2]{1,0:T(2,128)}, u32[]{:S(2)}) copy-start(s32[2,2]{1,0:T(2,128)} %param.12) | copy-start | bytes 52
  255.1 11.6 %copy-start.9 = (f32[2]{0:T(128)S(1)}, f32[2]{0:T(128)}, u32[]{:S(2)}) copy-start(f32[2]{0:T(128)} %param.13) | copy-start | bytes 28
  270.5 3.6 copy-start.10
  270.5 3.6 copy-start.4
  270.6 3.6 copy-start.7
  347.0 1.2 copy-start.11
  347.0 6.4 copy-start.5
  355.3 0.8 copy-start.1
  356.1 3.7 copy-start.2
  356.1 3.7 copy-start.3
  379.4 5.5 copy-start.6
  379.4 5.5 copy-start.12
  384.9 1.2 copy-start.11
  384.9 6.4 copy-start.5
  393.2 0.8 copy-start.1
  394.0 3.7 copy-start.2
  394.0 3.7 copy-start.3
  417.3 5.5 copy-start.6
  417.3 5.5 copy-start.12
  422.8 1.2 copy-start.11
  422.8 6.4 copy-start.5
  431.0 0.8 copy-start.1
  431.9 3.7 copy-start.2
  431.9 3.7 copy-start.3
  455.2 5.5 copy-start.6
  455.2 5.5 copy-start.12
  460.7 1.2 copy-start.11
  460.7 6.4 copy-start.5
  468.9 0.8 copy-start.1
  469.8 3.7 copy-start.2
  469.8 3.7 copy-start.3
  493.0 5.5 copy-start.6
  493.0 5.5 copy-start.12
  498.6 1.2 copy-start.11
  498.6 6.4 copy-start.5
  506.8 0.8 copy-start.1
  507.7 3.7 copy-start.2
  507.7 3.7 copy-start.3
  530.9 5.5 copy-start.6
  530.9 5.5 copy-start.12
  536.5 1.2 copy-start.11
  536.5 6.4 copy-start.5
  544.7 0.8 copy-start.1
  545.6 3.7 copy-start.2
  545.6 3.7 copy-start.3
  568.8 5.5 copy-start.6
  568.8 5.5 copy-start.12
  574.4 1.2 copy-start.11
  574.4 6.4 copy-start.5
  582.6 0.8 copy-start.1
  583.5 3.7 copy-start.2
  583.5 3.7 copy-start.3
  606.7 5.5 copy-start.6
  606.7 5.5 copy-start.12
  612.3 1.2 copy-start.11
  612.3 6.4 copy-start.5
  620.5 0.8 copy-start.1
  621.3 3.7 copy-start.2
  621.4 3.7 copy-start.3
  644.6 5.5 copy-start.6
  644.6 5.5 copy-start.12
Sparse Core Ops, SparseCore 0:
  11.7 2.2 sort.21.cloned.1.call-done
  (1 shorter events, 0.0 us)
Sparse Core Ops, SparseCore 1:
  274.1 64.8 all-reduce.1
where the time goes:
time: 668 us; the launch traced here: 663 us
  matrix products  255 us (38%)
  local copies, waits for them, and re-layouts  234 us (35%)
  other arithmetic  83.3 us (12%)
  waiting for transfers between devices  60.1 us (9%)
  between operations  15.7 us (2%)
  blocking collectives  9.31 us (1%)
    dot_general x8, matrix products, force_block(): smooth = jnp.dot(moments, form_table, precision=highest)  146 us
    psum x1, waiting for transfers between devices, shards(): summed = lax.psum(density_local, ('ka', 'ba'))  60.1 us
    unnamed x19, local copies, waits for them, and re-layouts  47.3 us
    reshape x1, local copies, waits for them, and re-layouts, shards(): coefficients.reshape(spin_count, complex_parts, kcount, bcount, atoms_blk...  45.4 us
    dot_general x8, matrix products, force_block(): return jnp.dot(smooth * wave_term, vectors, precision=highest)  44.3 us
    mul x1, local copies, waits for them, and re-layouts, shards(): masked = values * band_mask[:, None, :, :, None, None]  29.6 us
    dot_general x8, matrix products, force_block(): phases = jnp.dot(places, vectors.T, precision=highest)  29.6 us
    squeeze x2, local copies, waits for them, and re-layouts, shards(): masked[:, 1]  23.9 us
  transfers between devices with their start and end apart: 1, of which 1 were waited for; matrix products, arithmetic and copies ran while one was open for 1% of the time, Pallas kernels for 0%

commit v1 on v0

--- a/solution.py
+++ b/solution.py
@@ -90,7 +90,7 @@
     )
     ranking = jnp.argsort(owner_map.reshape(-1, atoms_blk), axis=1, stable=True)
     own_ranks = lax.dynamic_slice_in_dim(ranking, owner_index * per_owner, per_owner, 1)
-    summed = lax.psum(density_local, ("ka", "ba"))
+    summed = jnp.sum(jax.lax.all_gather(density_local, ("ka", "ba")), axis=0)
     own_rows = lax.dynamic_index_in_dim(own_ranks, group_index, 0, keepdims=False)
     own_density = jnp.take(summed, own_rows, axis=2)
     block_count = own_ranks.shape[0]

time: 668 us -> 716 us (1.072)
  waiting for transfers between devices: 60.1 us -> 98.4 us
  other arithmetic: 83.3 us -> 94.1 us
    all_gather x0 -> x1, waiting for transfers between devices: none -> 98.4 us  [shards(): summed = jnp.sum(jax.lax.all_gather(density_local, ('ka', 'ba')), axis=0)]
    psum x1 -> x0, waiting for transfers between devices: 60.1 us -> none  [shards(): summed = lax.psum(density_local, ('ka', 'ba'))]
    reduce_sum x0 -> x1, other arithmetic: none -> 10.8 us  [shards(): summed = jnp.sum(jax.lax.all_gather(density_local, ('ka', 'ba')), axis=0)]
where the time goes in v1:
time: 716 us; the launch traced here: 711 us
  matrix products  255 us (36%)
  local copies, waits for them, and re-layouts  233 us (33%)
  waiting for transfers between devices  98.4 us (14%)
  other arithmetic  94.1 us (13%)
  between operations  15.8 us (2%)
  blocking collectives  9.31 us (1%)
    dot_general x8, matrix products, force_block(): smooth = jnp.dot(moments, form_table, precision=highest)  146 us
    all_gather x1, waiting for transfers between devices, shards(): summed = jnp.sum(jax.lax.all_gather(density_local, ('ka', 'ba')), axis=0)  98.4 us
    unnamed x19, local copies, waits for them, and re-layouts  47.3 us
    reshape x1, local copies, waits for them, and re-layouts, shards(): coefficients.reshape(spin_count, complex_parts, kcount, bcount, atoms_blk...  45.4 us
    dot_general x8, matrix products, force_block(): return jnp.dot(smooth * wave_term, vectors, precision=highest)  44.2 us
    mul x1, local copies, waits for them, and re-layouts, shards(): masked = values * band_mask[:, None, :, :, None, None]  29.6 us
    dot_general x8, matrix products, force_block(): phases = jnp.dot(places, vectors.T, precision=highest)  29.6 us
    squeeze x2, local copies, waits for them, and re-layouts, shards(): masked[:, 1]  23.9 us
  transfers between devices with their start and end apart: 1, of which 1 were waited for; matrix products, arithmetic and copies ran while one was open for 1% of the time, Pallas kernels for 0%

profile of v1, /device:TPU:0, one launch (start us, length us, event | category | flops | bytes accessed | tf_op | source)
XLA Modules:
  0.0 710.6 jit_solution(487447894653610051)
XLA Ops:
  8.1 1.3 reshape.500
  10.0 45.7 %copy.44 = bf16[2,2,2,256,4608]{3,2,4,1,0:T(2,128)(2,1)} copy(bf16[2,2,2,256,4608]{4,3,2,1,0:T(8,128)(2,1)} %param.11) | data formatting | bytes 37748736 | tf_op args[0]
  55.7 45.4 %copy.45 = bf16[2,2,2,256,256,18]{4,3,5,2,1,0:T(8,128)(2,1)} copy(bf16[2,2,2,256,256,18]{3,2,5,4,1,0:T(2,128)(2,1)} %bitcast.68) | data formatting | bytes 37748736 | tf_op jit(solution)/shard_map/reshape | solution.py:78
  101.1 9.1 %slice.35 = bf16[2,1,2,256,256,18]{3,2,5,4,1,0:T(2,128)(2,1)} slice(bf16[2,2,2,256,256,18]{3,2,5,4,1,0:T(2,128)(2,1)} %bitcast.69), slice={[0:2], [0:1], [0:2], [0:256], [0:256], [0:18]} | slice | bytes 18874368 | tf_op jit(solution)/shard_map/slice | solution.py:84
  110.3 16.7 %broadcast_multiply_fusion.2 = bf16[2,2,2,256,256,18]{4,3,5,2,1,0:T(8,128)(2,1)} fusion(bf16[2,2,2,256,256,18]{4,3,5,2,1,0:T(8,128)(2,1)} %copy.45, bf16[2,2,256]{2,1,0:T(2,128)(2,1)S(1)} %compare_convert_fusion), kind=kLoop, calls=%fused_computation.84 | loop fusion | flops 9437184 | bytes 37750784 | tf_op jit(solution)/shard_map/mul | solution.py:79
  127.0 8.4 %slice_bitcast_fusion = bf16[2,2,256,256,18]{3,2,4,1,0:T(8,128)(2,1)} fusion(bf16[2,2,2,256,256,18]{4,3,5,2,1,0:T(8,128)(2,1)} %broadcast_multiply_fusion.2), kind=kLoop, calls=%fused_computation.83 | loop fusion | bytes 18874368 | tf_op jit(solution)/shard_map/squeeze | solution.py:84
  135.4 29.6 %copy.61 = bf16[2,2,2,256,256,18]{3,5,1,2,0,4:T(8,128)(2,1)} copy(bf16[2,2,2,256,256,18]{4,3,5,2,1,0:T(8,128)(2,1)} %broadcast_multiply_fusion.2) | data formatting | bytes 37748736 | tf_op jit(solution)/shard_map/mul | solution.py:79
  165.1 15.5 %copy.49 = bf16[2,2,256,256,18]{2,4,3,1,0:T(8,128)(2,1)} copy(bf16[2,2,256,256,18]{3,2,4,1,0:T(8,128)(2,1)} %slice_bitcast_fusion) | data formatting | bytes 18874368 | tf_op jit(solution)/shard_map/squeeze | solution.py:84
  180.6 13.3 %fusion.40 = f32[2,2,256,18,18]{4,3,2,1,0:T(8,128)} fusion(bf16[2,2,256,256,18]{2,4,3,1,0:T(8,128)(2,1)} %copy.49, bf16[2,1,2,256,256,18]{3,2,5,4,1,0:T(2,128)(2,1)} %slice.35), kind=kOutput, calls=%fused_computation.80 | convolution fusion | flops 169869312 | bytes 20201472 | tf_op jit(solution)/shard_map/skbai,skbaj->skaij/dot_general | solution.py:83
  193.9 14.0 %copy.50 = f32[2,2,256,18,18]{3,4,2,1,0:T(8,128)} copy(f32[2,2,256,18,18]{4,3,2,1,0:T(8,128)} %fusion.40) | data formatting | bytes 2654208 | tf_op jit(solution)/shard_map/skbai,skbaj->skaij/dot_general | solution.py:83
  207.9 14.1 %fusion.41 = f32[2,1,2,256,18,18]{5,4,3,2,0,1:T(8,128)} fusion(f32[2,2,256,18,18]{4,3,2,1,0:T(8,128)} %fusion.40, f32[2,2,256,18,18]{3,4,2,1,0:T(8,128)} %copy.50), kind=kLoop, calls=%fused_computation.82 | loop fusion | flops 331776 | bytes 3981312 | tf_op jit(solution)/shard_map/stack | solution.py:87
  221.9 11.4 %copy.52 = f32[2,1,2,256,18,18]{3,2,5,4,1,0:T(2,128)S(1)} copy(f32[2,1,2,256,18,18]{5,4,3,2,0,1:T(8,128)} %fusion.41) | data formatting | bytes 2654208 | tf_op jit(solution)/shard_map/stack | solution.py:87
  233.4 21.8 %fusion.42 = f32[2,1,2,256,18,18]{4,5,2,0,3,1:T(8,128)} fusion(bf16[2,2,2,256,256,18]{3,5,1,2,0,4:T(8,128)(2,1)} %copy.61, bf16[2,2,2,256,256,18]{3,2,5,4,1,0:T(2,128)(2,1)} %bitcast.70), kind=kOutput, calls=%fused_computation.85 | convolution fusion | flops 339738624 | bytes 39075840 | tf_op jit(solution)/shard_map/sckbai,sckbaj->skaij/dot_general | solution.py:80
  255.1 11.6 %copy.51 = f32[2,1,2,256,18,18]{3,2,5,4,1,0:T(2,128)S(1)} copy(f32[2,1,2,256,18,18]{4,5,2,0,3,1:T(8,128)} %fusion.42) | data formatting | bytes 2654208 | tf_op jit(solution)/shard_map/stack | solution.py:87
  266.8 3.7 fusion.45
  270.6 2.1 copy.54
  277.5 98.4 %all-gather.3.cloned.1.call-done = f32[8,2,2,256,324]{3,2,4,1,0:T(2,128)} async-done(((f32[1,2,2,256,324]{3,2,4,1,0:T(2,128)}), f32[8,2,2,256,324]{3,2,4,1,0:T(2,128)}) %all-gather.3.cloned.1.call-update) | async-done | bytes 10616848 | tf_op jit(solution)/shard_map/all_gather | solution.py:93
  375.9 10.8 %reduce_sum.28 = f32[2,2,256,324]{2,1,3,0:T(2,128)S(1)} reduce(f32[8,2,2,256,324]{3,2,4,1,0:T(2,128)} %all-gather.3.cloned.1.call-done, f32[]{:T(128)} %constant.178.clone.1), dimensions={0}, to_apply=%region_2.3 | reduce | flops 2322432 | bytes 11943940 | tf_op jit(solution)/shard_map/reduce_sum | solution.py:93
  386.7 1.3 copy.55
  390.0 4.4 all-gather
  394.5 303.1 %while.14 = (s32[]{:T(128)}, f32[64,3]{0,1:T(4,128)}, f32[2,1]{0,1:T(1,128)S(1)}, s32[8]{0:T(128)S(1)}, s32[]{:T(128)}, /*index=5*/f32[64,18]{0,1:T(8,128)S(1)},...) while((s32[]{:T(128)}, f32[64,3]{0,1:T(4,128)}, ...), condition=%wide.region_5.6_spmd.clone, body=%wide.region_4.5_spmd.clone.sunk | while | flops 262103424 | bytes 21960220 | solution.py:59
  398.7 1.2 add_subtract_fusion.2
  403.8 3.7 fusion.77
  407.5 1.3 dynamic-slice_reduce_fusion.3
  408.8 18.2 %convolution_multiply_fusion.3 = f32[13824,64]{0,1:T(8,128)} fusion(f32[18,13824]{1,0:T(8,128)} %mul.712, f32[64,18]{0,1:T(8,128)S(1)} %get-tuple-element.353, f32[13824,64]{0,1:T(8,128)S(1)} %fusion.77, f32[13824]{0:T(1024)S(1)} %get-tuple-element.318, f32[13824]{0:T(1024)S(1)} %get-tuple-element.319), kind=kOutput, calls=%fused_computation.3.clone.1 | convolution fusion | flops 194641920 | bytes 8188416 | tf_op jit(solution)/shard_map/while/body/eval_jaxpr/dot_general | solution.py:42
  427.0 5.5 convolution_add_fusion.2
  436.6 1.2 add_subtract_fusion.2
  439.2 1.2 mul.712
  441.6 3.7 fusion.77
  445.4 1.3 dynamic-slice_reduce_fusion.3
  446.7 18.2 %convolution_multiply_fusion.3 = f32[13824,64]{0,1:T(8,128)} fusion(f32[18,13824]{1,0:T(8,128)} %mul.712, f32[64,18]{0,1:T(8,128)S(1)} %get-tuple-element.353, f32[13824,64]{0,1:T(8,128)S(1)} %fusion.77, f32[13824]{0:T(1024)S(1)} %get-tuple-element.318, f32[13824]{0:T(1024)S(1)} %get-tuple-element.319), kind=kOutput, calls=%fused_computation.3.clone.1 | convolution fusion | flops 194641920 | bytes 8188416 | tf_op jit(solution)/shard_map/while/body/eval_jaxpr/dot_general | solution.py:42
  464.9 5.5 convolution_add_fusion.2
  474.5 1.2 add_subtract_fusion.2
  479.5 3.7 fusion.77
  483.2 1.3 dynamic-slice_reduce_fusion.3
  484.5 18.2 %convolution_multiply_fusion.3 = f32[13824,64]{0,1:T(8,128)} fusion(f32[18,13824]{1,0:T(8,128)} %mul.712, f32[64,18]{0,1:T(8,128)S(1)} %get-tuple-element.353, f32[13824,64]{0,1:T(8,128)S(1)} %fusion.77, f32[13824]{0:T(1024)S(1)} %get-tuple-element.318, f32[13824]{0:T(1024)S(1)} %get-tuple-element.319), kind=kOutput, calls=%fused_computation.3.clone.1 | convolution fusion | flops 194641920 | bytes 8188416 | tf_op jit(solution)/shard_map/while/body/eval_jaxpr/dot_general | solution.py:42
  502.7 5.5 convolution_add_fusion.2
  512.3 1.2 add_subtract_fusion.2
  517.3 3.7 fusion.77
  521.1 1.3 dynamic-slice_reduce_fusion.3
  522.4 18.2 %convolution_multiply_fusion.3 = f32[13824,64]{0,1:T(8,128)} fusion(f32[18,13824]{1,0:T(8,128)} %mul.712, f32[64,18]{0,1:T(8,128)S(1)} %get-tuple-element.353, f32[13824,64]{0,1:T(8,128)S(1)} %fusion.77, f32[13824]{0:T(1024)S(1)} %get-tuple-element.318, f32[13824]{0:T(1024)S(1)} %get-tuple-element.319), kind=kOutput, calls=%fused_computation.3.clone.1 | convolution fusion | flops 194641920 | bytes 8188416 | tf_op jit(solution)/shard_map/while/body/eval_jaxpr/dot_general | solution.py:42
  540.6 5.5 convolution_add_fusion.2
  550.2 1.2 add_subtract_fusion.2
  552.8 1.2 mul.712
  555.2 3.7 fusion.77
  558.9 1.3 dynamic-slice_reduce_fusion.3
  560.3 18.2 %convolution_multiply_fusion.3 = f32[13824,64]{0,1:T(8,128)} fusion(f32[18,13824]{1,0:T(8,128)} %mul.712, f32[64,18]{0,1:T(8,128)S(1)} %get-tuple-element.353, f32[13824,64]{0,1:T(8,128)S(1)} %fusion.77, f32[13824]{0:T(1024)S(1)} %get-tuple-element.318, f32[13824]{0:T(1024)S(1)} %get-tuple-element.319), kind=kOutput, calls=%fused_computation.3.clone.1 | convolution fusion | flops 194641920 | bytes 8188416 | tf_op jit(solution)/shard_map/while/body/eval_jaxpr/dot_general | solution.py:42
  578.5 5.5 convolution_add_fusion.2
  588.0 1.2 add_subtract_fusion.2
  593.1 3.7 fusion.77
  596.8 1.3 dynamic-slice_reduce_fusion.3
  598.1 18.2 %convolution_multiply_fusion.3 = f32[13824,64]{0,1:T(8,128)} fusion(f32[18,13824]{1,0:T(8,128)} %mul.712, f32[64,18]{0,1:T(8,128)S(1)} %get-tuple-element.353, f32[13824,64]{0,1:T(8,128)S(1)} %fusion.77, f32[13824]{0:T(1024)S(1)} %get-tuple-element.318, f32[13824]{0:T(1024)S(1)} %get-tuple-element.319), kind=kOutput, calls=%fused_computation.3.clone.1 | convolution fusion | flops 194641920 | bytes 8188416 | tf_op jit(solution)/shard_map/while/body/eval_jaxpr/dot_general | solution.py:42
  616.3 5.5 convolution_add_fusion.2
  625.9 1.2 add_subtract_fusion.2
  630.9 3.7 fusion.77
  634.7 1.3 dynamic-slice_reduce_fusion.3
  636.0 18.2 %convolution_multiply_fusion.3 = f32[13824,64]{0,1:T(8,128)} fusion(f32[18,13824]{1,0:T(8,128)} %mul.712, f32[64,18]{0,1:T(8,128)S(1)} %get-tuple-element.353, f32[13824,64]{0,1:T(8,128)S(1)} %fusion.77, f32[13824]{0:T(1024)S(1)} %get-tuple-element.318, f32[13824]{0:T(1024)S(1)} %get-tuple-element.319), kind=kOutput, calls=%fused_computation.3.clone.1 | convolution fusion | flops 194641920 | bytes 8188416 | tf_op jit(solution)/shard_map/while/body/eval_jaxpr/dot_general | solution.py:42
  654.2 5.5 convolution_add_fusion.2
  663.8 1.2 add_subtract_fusion.2
  668.8 3.7 fusion.77
  672.5 1.3 dynamic-slice_reduce_fusion.3
  673.8 18.2 %convolution_multiply_fusion.3 = f32[13824,64]{0,1:T(8,128)} fusion(f32[18,13824]{1,0:T(8,128)} %mul.712, f32[64,18]{0,1:T(8,128)S(1)} %get-tuple-element.353, f32[13824,64]{0,1:T(8,128)S(1)} %fusion.77, f32[13824]{0:T(1024)S(1)} %get-tuple-element.318, f32[13824]{0:T(1024)S(1)} %get-tuple-element.319), kind=kOutput, calls=%fused_computation.3.clone.1 | convolution fusion | flops 194641920 | bytes 8188416 | tf_op jit(solution)/shard_map/while/body/eval_jaxpr/dot_general | solution.py:42
  692.0 5.5 convolution_add_fusion.2
  697.6 4.9 psum.7
  (260 shorter events, 63.5 us)
Async XLA Ops:
  8.0 265.9 %copy-start = (s32[512]{0:T(512)S(1)}, s32[512]{0:T(512)}, u32[]{:S(2)}) copy-start(s32[512]{0:T(512)} %param.15) | copy-start | bytes 6148
  8.0 265.0 %sort.19.cloned.1.call-start = ((), (), s32[]{:S(2)}) async-start(), calls=%async_computation.1 | async-start | bytes 12320 | tf_op jit(solution)/shard_map/jit(argsort)/sort | solution.py:91
  9.9 365.9 %all-gather.3.cloned.1.call-start = ((), (), s32[]{:S(2)}) async-start(), calls=%async_computation | async-start | bytes 11943936 | tf_op jit(solution)/shard_map/all_gather | solution.py:93
  101.1 9.1 %copy-start.8 = (s32[2,2]{1,0:T(2,128)S(1)}, s32[2,2]{1,0:T(2,128)}, u32[]{:S(2)}) copy-start(s32[2,2]{1,0:T(2,128)} %param.12) | copy-start | bytes 52
  255.1 11.6 %copy-start.9 = (f32[2]{0:T(128)S(1)}, f32[2]{0:T(128)}, u32[]{:S(2)}) copy-start(f32[2]{0:T(128)} %param.13) | copy-start | bytes 28
  266.8 5.9 copy-start.4
  266.8 6.0 copy-start.7
  270.6 2.4 copy-start.10
  394.7 7.8 %copy-start.5 = (f32[2,1]{0,1:T(1,128)}, f32[2,1]{0,1:T(1,128)S(1)}, u32[]{:S(2)}) copy-start(f32[2,1]{0,1:T(1,128)S(1)} %get-tuple-element.350) | copy-start | bytes 28 | tf_op jit(solution)/shard_map/while
  394.7 7.8 %copy-start.11 = (s32[8]{0:T(128)}, s32[8]{0:T(128)S(1)}, u32[]{:S(2)}) copy-start(s32[8]{0:T(128)S(1)} %get-tuple-element.351) | copy-start | bytes 100 | tf_op jit(solution)/shard_map/while
  402.9 0.8 copy-start.1
  403.7 3.7 copy-start.2
  403.7 3.7 copy-start.3
  427.0 5.5 copy-start.6
  427.0 5.5 copy-start.12
  432.5 7.8 %copy-start.5 = (f32[2,1]{0,1:T(1,128)}, f32[2,1]{0,1:T(1,128)S(1)}, u32[]{:S(2)}) copy-start(f32[2,1]{0,1:T(1,128)S(1)} %get-tuple-element.350) | copy-start | bytes 28 | tf_op jit(solution)/shard_map/while
  432.5 7.8 %copy-start.11 = (s32[8]{0:T(128)}, s32[8]{0:T(128)S(1)}, u32[]{:S(2)}) copy-start(s32[8]{0:T(128)S(1)} %get-tuple-element.351) | copy-start | bytes 100 | tf_op jit(solution)/shard_map/while
  440.8 0.8 copy-start.1
  441.6 3.7 copy-start.2
  441.6 3.7 copy-start.3
  464.9 5.5 copy-start.6
  464.9 5.5 copy-start.12
  470.4 7.8 %copy-start.5 = (f32[2,1]{0,1:T(1,128)}, f32[2,1]{0,1:T(1,128)S(1)}, u32[]{:S(2)}) copy-start(f32[2,1]{0,1:T(1,128)S(1)} %get-tuple-element.350) | copy-start | bytes 28 | tf_op jit(solution)/shard_map/while
  470.4 7.8 %copy-start.11 = (s32[8]{0:T(128)}, s32[8]{0:T(128)S(1)}, u32[]{:S(2)}) copy-start(s32[8]{0:T(128)S(1)} %get-tuple-element.351) | copy-start | bytes 100 | tf_op jit(solution)/shard_map/while
  478.6 0.8 copy-start.1
  479.5 3.7 copy-start.2
  479.5 3.7 copy-start.3
  502.7 5.5 copy-start.6
  502.7 5.5 copy-start.12
  508.3 7.8 %copy-start.5 = (f32[2,1]{0,1:T(1,128)}, f32[2,1]{0,1:T(1,128)S(1)}, u32[]{:S(2)}) copy-start(f32[2,1]{0,1:T(1,128)S(1)} %get-tuple-element.350) | copy-start | bytes 28 | tf_op jit(solution)/shard_map/while
  508.3 7.8 %copy-start.11 = (s32[8]{0:T(128)}, s32[8]{0:T(128)S(1)}, u32[]{:S(2)}) copy-start(s32[8]{0:T(128)S(1)} %get-tuple-element.351) | copy-start | bytes 100 | tf_op jit(solution)/shard_map/while
  516.5 0.8 copy-start.1
  517.3 3.7 copy-start.2
  517.3 3.7 copy-start.3
  540.6 5.5 copy-start.6
  540.6 5.5 copy-start.12
  546.1 7.8 %copy-start.5 = (f32[2,1]{0,1:T(1,128)}, f32[2,1]{0,1:T(1,128)S(1)}, u32[]{:S(2)}) copy-start(f32[2,1]{0,1:T(1,128)S(1)} %get-tuple-element.350) | copy-start | bytes 28 | tf_op jit(solution)/shard_map/while
  546.1 7.8 %copy-start.11 = (s32[8]{0:T(128)}, s32[8]{0:T(128)S(1)}, u32[]{:S(2)}) copy-start(s32[8]{0:T(128)S(1)} %get-tuple-element.351) | copy-start | bytes 100 | tf_op jit(solution)/shard_map/while
  554.4 0.8 copy-start.1
  555.2 3.7 copy-start.2
  555.2 3.7 copy-start.3
  578.5 5.5 copy-start.6
  578.5 5.5 copy-start.12
  584.0 7.8 %copy-start.5 = (f32[2,1]{0,1:T(1,128)}, f32[2,1]{0,1:T(1,128)S(1)}, u32[]{:S(2)}) copy-start(f32[2,1]{0,1:T(1,128)S(1)} %get-tuple-element.350) | copy-start | bytes 28 | tf_op jit(solution)/shard_map/while
  584.0 7.8 %copy-start.11 = (s32[8]{0:T(128)}, s32[8]{0:T(128)S(1)}, u32[]{:S(2)}) copy-start(s32[8]{0:T(128)S(1)} %get-tuple-element.351) | copy-start | bytes 100 | tf_op jit(solution)/shard_map/while
  592.2 0.8 copy-start.1
  593.0 3.7 copy-start.2
  593.0 3.7 copy-start.3
  616.3 5.5 copy-start.6
  616.3 5.5 copy-start.12
  621.8 7.8 %copy-start.5 = (f32[2,1]{0,1:T(1,128)}, f32[2,1]{0,1:T(1,128)S(1)}, u32[]{:S(2)}) copy-start(f32[2,1]{0,1:T(1,128)S(1)} %get-tuple-element.350) | copy-start | bytes 28 | tf_op jit(solution)/shard_map/while
  621.8 7.8 %copy-start.11 = (s32[8]{0:T(128)}, s32[8]{0:T(128)S(1)}, u32[]{:S(2)}) copy-start(s32[8]{0:T(128)S(1)} %get-tuple-element.351) | copy-start | bytes 100 | tf_op jit(solution)/shard_map/while
  630.1 0.8 copy-start.1
  630.9 3.7 copy-start.2
  630.9 3.7 copy-start.3
  654.2 5.5 copy-start.6
  654.2 5.5 copy-start.12
  659.7 7.8 %copy-start.5 = (f32[2,1]{0,1:T(1,128)}, f32[2,1]{0,1:T(1,128)S(1)}, u32[]{:S(2)}) copy-start(f32[2,1]{0,1:T(1,128)S(1)} %get-tuple-element.350) | copy-start | bytes 28 | tf_op jit(solution)/shard_map/while
  659.7 7.8 %copy-start.11 = (s32[8]{0:T(128)}, s32[8]{0:T(128)S(1)}, u32[]{:S(2)}) copy-start(s32[8]{0:T(128)S(1)} %get-tuple-element.351) | copy-start | bytes 100 | tf_op jit(solution)/shard_map/while
  667.9 0.8 copy-start.1
  668.8 3.7 copy-start.2
  668.8 3.7 copy-start.3
  692.0 5.5 copy-start.6
  692.0 5.5 copy-start.12
Sparse Core Ops, SparseCore 0:
  11.7 2.2 sort.21.cloned.1.call-done
  (1 shorter events, 0.0 us)
Sparse Core Ops, SparseCore 1:
  272.8 103.0 all-gather.2
